TPU v7x, 32 devices: a whole 2x2x4 slice. The times are simulated.
32 devices in a mesh: groups: 2 (over y), freq: 4 (over z), space: 2 (over x), blk: 2 (over core).
Axes of the slice: x: 2, y: 2, z: 4, core: 2. Of those that a mesh axis runs over, the one named last changes fastest.
Arguments:
- realizations: bfloat16 [16, 64, 2, 8192], P('freq', 'groups', None, ('space', 'blk')), parts along dimension 1, may hold values from -6 to 6
- weights: float32 [16384], P(('groups', 'space', 'blk')), parts along dimension 0, may hold values from 0.25 to 4
- partners: int32 [3, 4], replicated, may hold values from 0 to 3, each once within a row
- block_count: int32 [2], P('groups'), parts along dimension 0, may hold values from 16 to 32
Outputs:
- modes: bfloat16 [16, 64, 2, 8192], P('freq', 'groups', None, ('space', 'blk')), parts along dimension 1
- gram: float32 [6, 16, 4, 2, 32, 32], P('groups', 'freq'), parts along dimension 0
There are 2 independent parts, one for each index of `groups`. A program takes and returns all parts, laid end to end along the dimension named above; an argument that names none is the same for every part. Nothing has to cross between parts.
Inputs may be any that keep to these rules, and one draw needn't show every extreme that they name: `partners`: each row is a permutation of the groups 0 to 3. `block_count`: blocks from this index on are left out.
All inputs are finite; a program needn't handle non-finite values.
Results may differ from a plain program's by a relative error of at most 0.0057.
Values may be sent and summed in bfloat16 or wider, within the bound.
A program may use at most 128 MiB of HBM per device.

v0:
```python
import jax
import jax.numpy as jnp
from jax import lax
from jax.sharding import PartitionSpec as P


def round_tables(partners, group_index, own_rows, which_round, per_group, total_freqs):
    offsets = jnp.arange(per_group, dtype=jnp.int32)
    partner_idx = partners[which_round, group_index] * per_group + offsets
    target_idx = (own_rows[:, None] + partner_idx[None, :]) % total_freqs
    return (partner_idx, target_idx)


def body(realizations, weights, partners, block_count):
    per_group = realizations.shape[0]
    blocks = realizations.shape[1]
    points = realizations.shape[3]
    rounds = partners.shape[0]
    shard_count = lax.axis_size("freq")
    total_freqs = per_group * shard_count
    total_space = points * lax.axis_size("space") * lax.axis_size("blk")
    gram_scale = 1.0 / jnp.sqrt(jnp.float32(total_space))
    mode_scale = 1.0 / jnp.sqrt(jnp.float32(rounds * per_group * blocks))
    keeper = (jnp.arange(blocks, dtype=jnp.int32) < block_count[0]).astype(jnp.bfloat16)
    fields = realizations * keeper[None, :, None, None]
    gathered = lax.all_gather(fields, "freq", axis=0, tiled=True)
    group_index = lax.axis_index("freq")
    own_rows = group_index * per_group + jnp.arange(per_group, dtype=jnp.int32)
    first = fields.astype(jnp.float32)[:, None]
    first_real = first[:, :, :, 0]
    first_imag = first[:, :, :, 1]
    round_grams = []
    for which_round in range(rounds):
        partner_idx, target_idx = round_tables(
            partners, group_index, own_rows, which_round, per_group, total_freqs
        )
        second = gathered[partner_idx].astype(jnp.float32)[None]
        real_part = first_real * second[:, :, :, 0] - first_imag * second[:, :, :, 1]
        imag_part = first_real * second[:, :, :, 1] + first_imag * second[:, :, :, 0]
        prod_real = (real_part * weights).astype(jnp.bfloat16)
        prod_imag = (imag_part * weights).astype(jnp.bfloat16)
        targets = gathered[target_idx]
        target_real = targets[:, :, :, 0]
        target_imag = targets[:, :, :, 1]
        real_gram = jnp.einsum(
            "ijas,ijbs->ijab", prod_real, target_real, preferred_element_type=jnp.float32
        ) + jnp.einsum(
            "ijas,ijbs->ijab", prod_imag, target_imag, preferred_element_type=jnp.float32
        )
        imag_gram = jnp.einsum(
            "ijas,ijbs->ijab", prod_real, target_imag, preferred_element_type=jnp.float32
        ) - jnp.einsum(
            "ijas,ijbs->ijab", prod_imag, target_real, preferred_element_type=jnp.float32
        )
        round_grams.append(jnp.stack([real_gram, imag_gram], axis=2))
    partial_value = jnp.stack(round_grams, axis=0)
    grams = lax.psum(partial_value, ("space", "blk")) * gram_scale
    accumulated = None
    for which_round in range(rounds):
        partner_idx, target_idx = round_tables(
            partners, group_index, own_rows, which_round, per_group, total_freqs
        )
        targets = gathered[target_idx]
        target_real = targets[:, :, :, 0]
        target_imag = targets[:, :, :, 1]
        rounded = grams[which_round].astype(jnp.bfloat16)
        real_mode = jnp.einsum(
            "ijab,ijbs->ias", rounded[:, :, 0], target_real, preferred_element_type=jnp.float32
        ) - jnp.einsum(
            "ijab,ijbs->ias", rounded[:, :, 1], target_imag, preferred_element_type=jnp.float32
        )
        imag_mode = jnp.einsum(
            "ijab,ijbs->ias", rounded[:, :, 0], target_imag, preferred_element_type=jnp.float32
        ) + jnp.einsum(
            "ijab,ijbs->ias", rounded[:, :, 1], target_real, preferred_element_type=jnp.float32
        )
        term = jnp.stack([real_mode, imag_mode], axis=2)
        accumulated = term if accumulated is None else accumulated + term
    modes = (accumulated * mode_scale).astype(jnp.bfloat16)
    return (modes, grams)


def solution(mesh):
    placed = (
        P("freq", "groups", None, ("space", "blk")),
        P(("groups", "space", "blk")),
        P(),
        P("groups"),
    )
    return jax.shard_map(
        body,
        mesh=mesh,
        in_specs=placed,
        out_specs=(
            P("freq", "groups", None, ("space", "blk")),
            P("groups", "freq", None, None, None, None),
        ),
        check_vma=False,
    )
```

profile of v0, /device:TPU:0, one launch (start us, length us, event | category | flops | bytes accessed | tf_op | source)
XLA Modules:
  0.0 216.9 jit_solution(5189849193543373611)
XLA Ops:
  7.9 2.8 %bitcast_convert_fusion.3 = (f32[4,1,32,2,2048]{4,2,3,0,1:T(8,128)S(1)}, bf16[4,32,2,2048]{3,1,2,0:T(8,128)(2,1)}) fusion(bf16[32]{0:T(256)(128)(2,1)S(1)} %compare_convert_fusion, bf16[4,32,2,2048]{3,2,1,0:T(2,128)(2,1)} %param.4), kind=kLoop, calls=%fused_computation.142 | loop fusion | flops 1048576 | bytes 4194368 | tf_op jit(solution)/shard_map/broadcast_in_dim | solution.py:29
  13.9 1.2 slice_bitcast_fusion.61
  15.1 79.3 %all-gather.2.cloned.1.call-done = bf16[16,32,2,2048]{3,1,2,0:T(8,128)(2,1)} async-done(((bf16[4,32,2,2048]{3,1,2,0:T(8,128)(2,1)}), bf16[16,32,2,2048]{3,1,2,0:T(8,128)(2,1)}) %all-gather.2.cloned.1.call-update) | async-done | bytes 4194320 | tf_op jit(solution)/shard_map/all_gather | solution.py:26
  94.4 2.8 %gather_fusion.4 = bf16[4,32,2,2048]{3,1,2,0:T(8,128)(2,1)S(1)} fusion(bf16[16,32,2,2048]{3,1,2,0:T(8,128)(2,1)} %all-gather.2.cloned.1.call-done, s32[1024]{0:T(1024)S(1)} %pad_clamp_fusion.1), kind=kCustom, calls=%fused_computation.4 | custom fusion | bytes 2097168 | tf_op jit(solution)/shard_map/gather | solution.py:37
  97.4 1.2 slice_bitcast_fusion.55
  98.6 5.4 %gather_fusion.5 = bf16[16,32,2,2048]{3,1,2,0:T(8,128)(2,1)} fusion(bf16[16,32,2,2048]{3,1,2,0:T(8,128)(2,1)} %all-gather.2.cloned.1.call-done, s32[1024]{0:T(1024)S(1)} %pad_clamp_fusion), kind=kCustom, calls=%fused_computation.5 | custom fusion | bytes 8388672 | tf_op jit(solution)/shard_map/gather | solution.py:42
  104.0 2.6 %copy.14 = bf16[16,32,2,2048]{3,1,0,2:T(8,128)(2,1)S(1)} copy(bf16[16,32,2,2048]{3,1,2,0:T(8,128)(2,1)} %gather_fusion.5) | data formatting | bytes 8388608 | tf_op jit(solution)/shard_map/gather | solution.py:42
  106.8 1.9 fusion.20
  108.7 1.2 fusion.21
  109.9 2.8 %gather_fusion.2 = bf16[4,32,2,2048]{3,1,2,0:T(8,128)(2,1)S(1)} fusion(bf16[16,32,2,2048]{3,1,2,0:T(8,128)(2,1)} %all-gather.2.cloned.1.call-done, s32[1024]{0:T(1024)S(1)} %pad_clamp_fusion.3), kind=kCustom, calls=%fused_computation.2 | custom fusion | bytes 2097168 | tf_op jit(solution)/shard_map/gather | solution.py:37
  113.0 1.2 slice_bitcast_fusion.57
  114.2 5.4 %gather_fusion.3 = bf16[16,32,2,2048]{3,1,2,0:T(8,128)(2,1)} fusion(bf16[16,32,2,2048]{3,1,2,0:T(8,128)(2,1)} %all-gather.2.cloned.1.call-done, s32[1024]{0:T(1024)S(1)} %pad_clamp_fusion.2), kind=kCustom, calls=%fused_computation.3 | custom fusion | bytes 8388672 | tf_op jit(solution)/shard_map/gather | solution.py:42
  119.6 2.6 %copy.13 = bf16[16,32,2,2048]{3,1,0,2:T(8,128)(2,1)S(1)} copy(bf16[16,32,2,2048]{3,1,2,0:T(8,128)(2,1)} %gather_fusion.3) | data formatting | bytes 8388608 | tf_op jit(solution)/shard_map/gather | solution.py:42
  122.2 2.0 fusion.16
  124.2 1.9 fusion.17
  126.1 2.8 %gather_fusion = bf16[4,32,2,2048]{3,1,2,0:T(8,128)(2,1)S(1)} fusion(bf16[16,32,2,2048]{3,1,2,0:T(8,128)(2,1)} %all-gather.2.cloned.1.call-done, s32[1024]{0:T(1024)S(1)} %pad_clamp_fusion.5), kind=kCustom, calls=%fused_computation | custom fusion | bytes 2097168 | tf_op jit(solution)/shard_map/gather | solution.py:37
  129.2 1.2 slice_bitcast_fusion.60
  130.4 4.9 %gather_fusion.1 = bf16[16,32,2,2048]{3,1,2,0:T(8,128)(2,1)} fusion(bf16[16,32,2,2048]{3,1,2,0:T(8,128)(2,1)} %all-gather.2.cloned.1.call-done, s32[1024]{0:T(1024)S(1)} %pad_clamp_fusion.4), kind=kCustom, calls=%fused_computation.1 | custom fusion | bytes 8388672 | tf_op jit(solution)/shard_map/gather | solution.py:42
  135.3 2.6 %copy.12 = bf16[16,32,2,2048]{3,1,0,2:T(8,128)(2,1)S(1)} copy(bf16[16,32,2,2048]{3,1,2,0:T(8,128)(2,1)} %gather_fusion.1) | data formatting | bytes 8388608 | tf_op jit(solution)/shard_map/gather | solution.py:42
  137.9 1.2 fusion.12
  139.2 1.2 fusion.13
  142.1 1.4 fusion.90
  143.6 1.7 fusion.88
  146.4 1.3 fusion.94
  147.7 1.9 fusion.92
  149.6 1.2 fusion.98
  150.8 1.6 fusion.96
  152.6 1.4 pad_maximum_fusion
  154.0 41.5 %all-reduce.2.cloned.1.call-done = f32[3,4,4,2,32,32]{5,4,2,1,3,0:T(8,128)} async-done(((f32[3,4,4,2,32,32]{5,4,2,1,3,0:T(8,128)}), f32[3,4,4,2,32,32]{5,4,2,1,3,0:T(8,128)}) %all-reduce.2.cloned.1.call-update) | async-done | bytes 393232 | tf_op jit(solution)/shard_map/psum | solution.py:57
  195.5 1.8 broadcast_multiply_fusion
  202.4 1.3 copy.16
  208.0 2.0 copy.15
  (87 shorter events, 14.4 us)
Async XLA Ops:
  7.2 3.6 %copy-start.18 = (s32[3,4]{1,0:T(4,128)S(1)}, s32[3,4]{1,0:T(4,128)}, u32[]{:S(2)}) copy-start(s32[3,4]{1,0:T(4,128)} %param.6) | copy-start | bytes 148
  7.2 87.2 %all-gather.2.cloned.1.call-start = ((), (), s32[]{:S(2)}) async-start(), calls=%async_computation | async-start | bytes 5242880 | tf_op jit(solution)/shard_map/all_gather | solution.py:26
  10.8 184.7 %all-reduce.2.cloned.1.call-start = ((), (), s32[]{:S(2)}) async-start(), calls=%async_computation.1 | async-start | bytes 3145728 | tf_op jit(solution)/shard_map/psum | solution.py:57
  98.6 10.1 %copy-start.9 = (f32[4,32,2048]{2,1,0:T(8,128)}, f32[4,32,2048]{2,1,0:T(8,128)S(1)}, u32[]{:S(2)}) copy-start(f32[4,32,2048]{2,1,0:T(8,128)S(1)} %get-tuple-element.14) | copy-start | bytes 3145732
  104.0 2.7 %copy-start.8 = (f32[4,32,2048]{2,1,0:T(8,128)S(1)}, f32[4,32,2048]{2,1,0:T(8,128)}, u32[]{:S(2)}) copy-start(f32[4,32,2048]{2,1,0:T(8,128)} %get-tuple-element.13) | copy-start | bytes 3145732
  104.0 2.8 %copy-start.11 = (f32[4,32,2048]{2,1,0:T(8,128)S(1)}, f32[4,32,2048]{2,1,0:T(8,128)}, u32[]{:S(2)}) copy-start(f32[4,32,2048]{2,1,0:T(8,128)} %get-tuple-element.15) | copy-start | bytes 3145732
  104.0 2.8 %copy-start.19 = (f32[2048]{0:T(1024)S(1)}, f32[2048]{0:T(1024)}, u32[]{:S(2)}) copy-start(f32[2048]{0:T(1024)} %param.5) | copy-start | bytes 24580
  106.6 2.1 copy-start
  114.2 10.0 %copy-start.13 = (f32[4,32,2048]{2,1,0:T(8,128)}, f32[4,32,2048]{2,1,0:T(8,128)S(1)}, u32[]{:S(2)}) copy-start(f32[4,32,2048]{2,1,0:T(8,128)S(1)} %get-tuple-element.10) | copy-start | bytes 3145732
  119.5 2.6 %copy-start.15 = (f32[4,32,2048]{2,1,0:T(8,128)S(1)}, f32[4,32,2048]{2,1,0:T(8,128)}, u32[]{:S(2)}) copy-start(f32[4,32,2048]{2,1,0:T(8,128)} %get-tuple-element.11) | copy-start | bytes 3145732
  122.1 2.1 copy-start.3
  135.3 2.6 %copy-start.17 = (f32[4,32,2048]{2,1,0:T(8,128)S(1)}, f32[4,32,2048]{2,1,0:T(8,128)}, u32[]{:S(2)}) copy-start(f32[4,32,2048]{2,1,0:T(8,128)} %get-tuple-element.9) | copy-start | bytes 3145732
  137.9 12.9 %copy-start.6 = (bf16[16,32,2,2048]{3,1,0,2:T(8,128)(2,1)}, bf16[16,32,2,2048]{3,1,0,2:T(8,128)(2,1)S(1)}, u32[]{:S(2)}) copy-start(bf16[16,32,2,2048]{3,1,0,2:T(8,128)(2,1)S(1)} %copy.12) | copy-start | bytes 12582916
  139.2 2.4 %copy-start.1 = (bf16[16,32,2,2048]{3,1,0,2:T(8,128)(2,1)S(1)}, bf16[16,32,2,2048]{3,1,0,2:T(8,128)(2,1)}, u32[]{:S(2)}) copy-start(bf16[16,32,2,2048]{3,1,0,2:T(8,128)(2,1)} %copy-done) | copy-start | bytes 12582916
  139.2 2.6 %copy-start.10 = (f32[4,32,2048]{2,1,0:T(8,128)S(1)}, f32[4,32,2048]{2,1,0:T(8,128)}, u32[]{:S(2)}) copy-start(f32[4,32,2048]{2,1,0:T(8,128)} %copy-done.9) | copy-start | bytes 3145732
  139.2 3.0 %copy-start.12 = (f32[4,32,2048]{2,1,0:T(8,128)S(1)}, f32[4,32,2048]{2,1,0:T(8,128)}, u32[]{:S(2)}) copy-start(f32[4,32,2048]{2,1,0:T(8,128)} %get-tuple-element.15) | copy-start | bytes 3145732
  139.2 3.0 %copy-start.20 = (f32[4,4,32,32]{3,2,1,0:T(8,128)S(1)}, f32[4,4,32,32]{3,2,1,0:T(8,128)}, u32[]{:S(2)}) copy-start(f32[4,4,32,32]{3,2,1,0:T(8,128)} %fusion.20) | copy-start | bytes 196612
  143.5 2.2 %copy-start.4 = (bf16[16,32,2,2048]{3,1,0,2:T(8,128)(2,1)S(1)}, bf16[16,32,2,2048]{3,1,0,2:T(8,128)(2,1)}, u32[]{:S(2)}) copy-start(bf16[16,32,2,2048]{3,1,0,2:T(8,128)(2,1)} %copy-done.3) | copy-start | bytes 12582916
  143.5 2.5 %copy-start.14 = (f32[4,32,2048]{2,1,0:T(8,128)S(1)}, f32[4,32,2048]{2,1,0:T(8,128)}, u32[]{:S(2)}) copy-start(f32[4,32,2048]{2,1,0:T(8,128)} %copy-done.13) | copy-start | bytes 3145732
  143.6 2.8 %copy-start.16 = (f32[4,32,2048]{2,1,0:T(8,128)S(1)}, f32[4,32,2048]{2,1,0:T(8,128)}, u32[]{:S(2)}) copy-start(f32[4,32,2048]{2,1,0:T(8,128)} %get-tuple-element.11) | copy-start | bytes 3145732
  143.6 2.8 %copy-start.22 = (f32[4,4,32,32]{3,2,1,0:T(8,128)S(1)}, f32[4,4,32,32]{3,2,1,0:T(8,128)}, u32[]{:S(2)}) copy-start(f32[4,4,32,32]{3,2,1,0:T(8,128)} %fusion.16) | copy-start | bytes 196612
  146.4 1.3 copy-start.21
  195.5 2.7 %copy-start.2 = (bf16[16,32,2,2048]{3,1,0,2:T(8,128)(2,1)S(1)}, bf16[16,32,2,2048]{3,1,0,2:T(8,128)(2,1)}, u32[]{:S(2)}) copy-start(bf16[16,32,2,2048]{3,1,0,2:T(8,128)(2,1)} %copy-done) | copy-start | bytes 12582916
  197.3 2.4 %copy-start.5 = (bf16[16,32,2,2048]{3,1,0,2:T(8,128)(2,1)S(1)}, bf16[16,32,2,2048]{3,1,0,2:T(8,128)(2,1)}, u32[]{:S(2)}) copy-start(bf16[16,32,2,2048]{3,1,0,2:T(8,128)(2,1)} %copy-done.3) | copy-start | bytes 12582916
  198.7 2.4 %copy-start.7 = (bf16[16,32,2,2048]{3,1,0,2:T(8,128)(2,1)S(1)}, bf16[16,32,2,2048]{3,1,0,2:T(8,128)(2,1)}, u32[]{:S(2)}) copy-start(bf16[16,32,2,2048]{3,1,0,2:T(8,128)(2,1)} %copy-done.6) | copy-start | bytes 12582916
Sparse Core Ops, SparseCore 0:
  10.9 83.4 all-gather.1
  154.1 41.3 all-reduce.1
where the time goes:
time: 217 us
  waiting for transfers between devices  121 us (56%)
  local copies, waits for them, and re-layouts  45.3 us (21%)
  matrix products  25.9 us (12%)
  between operations  17 us (8%)
  other arithmetic  7.77 us (4%)
    all_gather x1, waiting for transfers between devices, body(): gathered = lax.all_gather(fields, 'freq', axis=0, tiled=True)  79.3 us
    psum x1, waiting for transfers between devices, body(): grams = lax.psum(partial_value, ('space', 'blk')) * gram_scale  41.5 us
    gather x6, local copies, waits for them, and re-layouts, body(): targets = gathered[target_idx]  23.5 us
    gather x3, local copies, waits for them, and re-layouts, body(): second = gathered[partner_idx].astype(jnp.float32)[None]  8.4 us
    unnamed x48, local copies, waits for them, and re-layouts  7.75 us
    dot_general x3, matrix products, body(): jnp.einsum('ijas,ijbs->ijab', prod_real, target_imag, preferred_element_t...  5.19 us
    dot_general x3, matrix products, body(): jnp.einsum('ijas,ijbs->ijab', prod_imag, target_imag, preferred_element_t...  5.13 us
    mul x4, local copies, waits for them, and re-layouts, body(): first_real * second[:, :, :, 0] - first_imag * second[:, :, :, 1]  4.69 us
  transfers between devices with their start and end apart: 2, of which 2 were waited for; matrix products, arithmetic and copies ran while one was open for 1% of the time, Pallas kernels for 0%

commit v1 on v0

--- a/solution.py
+++ b/solution.py
@@ -2,6 +2,12 @@
 import jax.numpy as jnp
 from jax import lax
 from jax.sharding import PartitionSpec as P
+
+
+def summed_here(x, axis):
+    pieces = lax.all_gather(x, axis, axis=0, tiled=False)
+    result = pieces.sum(axis=0)
+    return result
 
 
 def round_tables(partners, group_index, own_rows, which_round, per_group, total_freqs):
@@ -54,7 +60,7 @@
         )
         round_grams.append(jnp.stack([real_gram, imag_gram], axis=2))
     partial_value = jnp.stack(round_grams, axis=0)
-    grams = lax.psum(partial_value, ("space", "blk")) * gram_scale
+    grams = summed_here(partial_value, ("space", "blk")) * gram_scale
     accumulated = None
     for which_round in range(rounds):
         partner_idx, target_idx = round_tables(

time: 217 us -> 225 us (1.037)
  waiting for transfers between devices: 121 us -> 124 us
  local copies, waits for them, and re-layouts: 45.3 us -> 47.8 us
    all_gather x0 -> x1, waiting for transfers between devices: none -> 45.1 us  [summed_here(): pieces = lax.all_gather(x, axis, axis=0, tiled=False)]
    psum x1 -> x0, waiting for transfers between devices: 41.5 us -> none  [body(): grams = lax.psum(partial_value, ('space', 'blk')) * gram_scale]
    reduce_sum x0 -> x1, other arithmetic: none -> 3.8 us  [summed_here(): result = pieces.sum(axis=0)]
where the time goes in v1:
time: 225 us; the launch traced here: 224 us
  waiting for transfers between devices  124 us (55%)
  local copies, waits for them, and re-layouts  47.8 us (21%)
  matrix products  26 us (12%)
  between operations  17.1 us (8%)
  other arithmetic  8.87 us (4%)
    all_gather x1, waiting for transfers between devices, body(): gathered = lax.all_gather(fields, 'freq', axis=0, tiled=True)  79.3 us
    all_gather x1, waiting for transfers between devices, summed_here(): pieces = lax.all_gather(x, axis, axis=0, tiled=False)  45.1 us
    gather x6, local copies, waits for them, and re-layouts, body(): targets = gathered[target_idx]  23.6 us
    unnamed x48, local copies, waits for them, and re-layouts  8.77 us
    gather x3, local copies, waits for them, and re-layouts, body(): second = gathered[partner_idx].astype(jnp.float32)[None]  8.4 us
    dot_general x3, matrix products, body(): jnp.einsum('ijas,ijbs->ijab', prod_real, target_imag, preferred_element_t...  5.3 us
    dot_general x3, matrix products, body(): jnp.einsum('ijas,ijbs->ijab', prod_imag, target_imag, preferred_element_t...  5.13 us
    mul x4, local copies, waits for them, and re-layouts, body(): first_real * second[:, :, :, 0] - first_imag * second[:, :, :, 1]  4.68 us
  transfers between devices with their start and end apart: 2, of which 2 were waited for; matrix products, arithmetic and copies ran while one was open for 1% of the time, Pallas kernels for 0%

profile of v1, /device:TPU:0, one launch (start us, length us, event | category | flops | bytes accessed | tf_op | source)
XLA Modules:
  0.0 224.1 jit_solution(9929250113062392584)
XLA Ops:
  7.9 2.8 %bitcast_convert_fusion.3 = (f32[4,1,32,2,2048]{4,2,3,0,1:T(8,128)S(1)}, bf16[4,32,2,2048]{3,1,2,0:T(8,128)(2,1)}) fusion(bf16[32]{0:T(256)(128)(2,1)S(1)} %compare_convert_fusion, bf16[4,32,2,2048]{3,2,1,0:T(2,128)(2,1)} %param.4), kind=kLoop, calls=%fused_computation.143 | loop fusion | flops 1048576 | bytes 4194368 | tf_op jit(solution)/shard_map/broadcast_in_dim | solution.py:35
  15.1 79.3 %all-gather.4.cloned.1.call-done = bf16[16,32,2,2048]{3,1,2,0:T(8,128)(2,1)} async-done(((bf16[4,32,2,2048]{3,1,2,0:T(8,128)(2,1)}), bf16[16,32,2,2048]{3,1,2,0:T(8,128)(2,1)}) %all-gather.4.cloned.1.call-update) | async-done | bytes 4194320 | tf_op jit(solution)/shard_map/all_gather | solution.py:32
  94.4 2.8 %gather_fusion.4 = bf16[4,32,2,2048]{3,1,2,0:T(8,128)(2,1)S(1)} fusion(bf16[16,32,2,2048]{3,1,2,0:T(8,128)(2,1)} %all-gather.4.cloned.1.call-done, s32[1024]{0:T(1024)S(1)} %pad_clamp_fusion.1), kind=kCustom, calls=%fused_computation.4 | custom fusion | bytes 2097168 | tf_op jit(solution)/shard_map/gather | solution.py:43
  97.4 1.2 slice_bitcast_fusion.55
  98.6 5.4 %gather_fusion.5 = bf16[16,32,2,2048]{3,1,2,0:T(8,128)(2,1)} fusion(bf16[16,32,2,2048]{3,1,2,0:T(8,128)(2,1)} %all-gather.4.cloned.1.call-done, s32[1024]{0:T(1024)S(1)} %pad_clamp_fusion), kind=kCustom, calls=%fused_computation.5 | custom fusion | bytes 8388672 | tf_op jit(solution)/shard_map/gather | solution.py:48
  104.0 2.6 %copy.21 = bf16[16,32,2,2048]{3,1,0,2:T(8,128)(2,1)S(1)} copy(bf16[16,32,2,2048]{3,1,2,0:T(8,128)(2,1)} %gather_fusion.5) | data formatting | bytes 8388608 | tf_op jit(solution)/shard_map/gather | solution.py:48
  106.8 2.0 fusion.20
  108.8 1.2 fusion.21
  110.0 2.8 %gather_fusion.2 = bf16[4,32,2,2048]{3,1,2,0:T(8,128)(2,1)S(1)} fusion(bf16[16,32,2,2048]{3,1,2,0:T(8,128)(2,1)} %all-gather.4.cloned.1.call-done, s32[1024]{0:T(1024)S(1)} %pad_clamp_fusion.3), kind=kCustom, calls=%fused_computation.2 | custom fusion | bytes 2097168 | tf_op jit(solution)/shard_map/gather | solution.py:43
  113.1 1.2 slice_bitcast_fusion.57
  114.3 5.4 %gather_fusion.3 = bf16[16,32,2,2048]{3,1,2,0:T(8,128)(2,1)} fusion(bf16[16,32,2,2048]{3,1,2,0:T(8,128)(2,1)} %all-gather.4.cloned.1.call-done, s32[1024]{0:T(1024)S(1)} %pad_clamp_fusion.2), kind=kCustom, calls=%fused_computation.3 | custom fusion | bytes 8388672 | tf_op jit(solution)/shard_map/gather | solution.py:48
  119.7 2.6 %copy.20 = bf16[16,32,2,2048]{3,1,0,2:T(8,128)(2,1)S(1)} copy(bf16[16,32,2,2048]{3,1,2,0:T(8,128)(2,1)} %gather_fusion.3) | data formatting | bytes 8388608 | tf_op jit(solution)/shard_map/gather | solution.py:48
  122.3 2.1 fusion.16
  124.4 1.9 fusion.17
  126.3 2.8 %gather_fusion = bf16[4,32,2,2048]{3,1,2,0:T(8,128)(2,1)S(1)} fusion(bf16[16,32,2,2048]{3,1,2,0:T(8,128)(2,1)} %all-gather.4.cloned.1.call-done, s32[1024]{0:T(1024)S(1)} %pad_clamp_fusion.5), kind=kCustom, calls=%fused_computation | custom fusion | bytes 2097168 | tf_op jit(solution)/shard_map/gather | solution.py:43
  129.4 1.2 slice_bitcast_fusion.60
  130.5 5.0 %gather_fusion.1 = bf16[16,32,2,2048]{3,1,2,0:T(8,128)(2,1)} fusion(bf16[16,32,2,2048]{3,1,2,0:T(8,128)(2,1)} %all-gather.4.cloned.1.call-done, s32[1024]{0:T(1024)S(1)} %pad_clamp_fusion.4), kind=kCustom, calls=%fused_computation.1 | custom fusion | bytes 8388672 | tf_op jit(solution)/shard_map/gather | solution.py:48
  135.5 2.6 %copy.19 = bf16[16,32,2,2048]{3,1,0,2:T(8,128)(2,1)S(1)} copy(bf16[16,32,2,2048]{3,1,2,0:T(8,128)(2,1)} %gather_fusion.1) | data formatting | bytes 8388608 | tf_op jit(solution)/shard_map/gather | solution.py:48
  138.1 1.2 fusion.12
  139.4 1.2 fusion.13
  142.4 1.4 fusion.90
  143.8 1.7 fusion.88
  146.6 1.3 fusion.94
  147.9 1.9 fusion.92
  149.8 1.2 fusion.98
  151.0 1.6 fusion.96
  153.0 1.3 copy.22
  154.3 45.1 %all-gather.6.cloned.1.call-done = f32[12,4,4,2,32,32]{5,4,3,2,1,0:T(8,128)} async-done(((f32[3,4,4,2,32,32]{5,4,3,2,1,0:T(8,128)}), f32[12,4,4,2,32,32]{5,4,3,2,1,0:T(8,128)}) %all-gather.6.cloned.1.call-update) | async-done | bytes 1572880 | tf_op jit(solution)/shard_map/all_gather | solution.py:8
  199.4 3.8 %reduce_sum.9 = f32[3,4,4,2,32,32]{5,4,3,2,1,0:T(8,128)S(1)} reduce(f32[4,3,4,4,2,32,32]{6,5,4,3,2,1,0:T(8,128)} %bitcast.253, f32[]{:T(128)} %constant.57.clone.1), dimensions={0}, to_apply=%region_0.1 | reduce | flops 294912 | bytes 1966084 | tf_op jit(solution)/shard_map/reduce_sum | solution.py:9
  203.6 1.8 copy-done.2
  209.6 1.3 copy.25
  215.2 2.0 copy.24
  (89 shorter events, 15.3 us)
Async XLA Ops:
  7.2 3.6 %copy-start.18 = (s32[3,4]{1,0:T(4,128)S(1)}, s32[3,4]{1,0:T(4,128)}, u32[]{:S(2)}) copy-start(s32[3,4]{1,0:T(4,128)} %param.6) | copy-start | bytes 148
  7.2 87.2 %all-gather.4.cloned.1.call-start = ((), (), s32[]{:S(2)}) async-start(), calls=%async_computation | async-start | bytes 5242880 | tf_op jit(solution)/shard_map/all_gather | solution.py:32
  10.8 188.7 %all-gather.6.cloned.1.call-start = ((), (), s32[]{:S(2)}) async-start(), calls=%async_computation.1 | async-start | bytes 7864320 | tf_op jit(solution)/shard_map/all_gather | solution.py:8
  98.6 10.2 %copy-start.9 = (f32[4,32,2048]{2,1,0:T(8,128)}, f32[4,32,2048]{2,1,0:T(8,128)S(1)}, u32[]{:S(2)}) copy-start(f32[4,32,2048]{2,1,0:T(8,128)S(1)} %get-tuple-element.16) | copy-start | bytes 3145732
  104.0 2.7 %copy-start.8 = (f32[4,32,2048]{2,1,0:T(8,128)S(1)}, f32[4,32,2048]{2,1,0:T(8,128)}, u32[]{:S(2)}) copy-start(f32[4,32,2048]{2,1,0:T(8,128)} %get-tuple-element.15) | copy-start | bytes 3145732
  104.0 2.8 %copy-start.11 = (f32[4,32,2048]{2,1,0:T(8,128)S(1)}, f32[4,32,2048]{2,1,0:T(8,128)}, u32[]{:S(2)}) copy-start(f32[4,32,2048]{2,1,0:T(8,128)} %get-tuple-element.17) | copy-start | bytes 3145732
  104.0 2.8 %copy-start.19 = (f32[2048]{0:T(1024)S(1)}, f32[2048]{0:T(1024)}, u32[]{:S(2)}) copy-start(f32[2048]{0:T(1024)} %param.5) | copy-start | bytes 24580
  106.6 2.2 copy-start
  114.3 10.1 %copy-start.13 = (f32[4,32,2048]{2,1,0:T(8,128)}, f32[4,32,2048]{2,1,0:T(8,128)S(1)}, u32[]{:S(2)}) copy-start(f32[4,32,2048]{2,1,0:T(8,128)S(1)} %get-tuple-element.12) | copy-start | bytes 3145732
  119.7 2.6 %copy-start.15 = (f32[4,32,2048]{2,1,0:T(8,128)S(1)}, f32[4,32,2048]{2,1,0:T(8,128)}, u32[]{:S(2)}) copy-start(f32[4,32,2048]{2,1,0:T(8,128)} %get-tuple-element.13) | copy-start | bytes 3145732
  122.3 2.1 copy-start.3
  135.5 2.6 %copy-start.17 = (f32[4,32,2048]{2,1,0:T(8,128)S(1)}, f32[4,32,2048]{2,1,0:T(8,128)}, u32[]{:S(2)}) copy-start(f32[4,32,2048]{2,1,0:T(8,128)} %get-tuple-element.11) | copy-start | bytes 3145732
  138.1 12.9 %copy-start.6 = (bf16[16,32,2,2048]{3,1,0,2:T(8,128)(2,1)}, bf16[16,32,2,2048]{3,1,0,2:T(8,128)(2,1)S(1)}, u32[]{:S(2)}) copy-start(bf16[16,32,2,2048]{3,1,0,2:T(8,128)(2,1)S(1)} %copy.19) | copy-start | bytes 12582916
  139.4 2.4 %copy-start.1 = (bf16[16,32,2,2048]{3,1,0,2:T(8,128)(2,1)S(1)}, bf16[16,32,2,2048]{3,1,0,2:T(8,128)(2,1)}, u32[]{:S(2)}) copy-start(bf16[16,32,2,2048]{3,1,0,2:T(8,128)(2,1)} %copy-done) | copy-start | bytes 12582916
  139.4 2.7 %copy-start.10 = (f32[4,32,2048]{2,1,0:T(8,128)S(1)}, f32[4,32,2048]{2,1,0:T(8,128)}, u32[]{:S(2)}) copy-start(f32[4,32,2048]{2,1,0:T(8,128)} %copy-done.9) | copy-start | bytes 3145732
  139.4 3.0 %copy-start.12 = (f32[4,32,2048]{2,1,0:T(8,128)S(1)}, f32[4,32,2048]{2,1,0:T(8,128)}, u32[]{:S(2)}) copy-start(f32[4,32,2048]{2,1,0:T(8,128)} %get-tuple-element.17) | copy-start | bytes 3145732
  139.4 3.0 %copy-start.20 = (f32[4,4,32,32]{3,2,1,0:T(8,128)S(1)}, f32[4,4,32,32]{3,2,1,0:T(8,128)}, u32[]{:S(2)}) copy-start(f32[4,4,32,32]{3,2,1,0:T(8,128)} %fusion.20) | copy-start | bytes 196612
  143.7 2.2 copy-start.4
  143.8 2.5 %copy-start.14 = (f32[4,32,2048]{2,1,0:T(8,128)S(1)}, f32[4,32,2048]{2,1,0:T(8,128)}, u32[]{:S(2)}) copy-start(f32[4,32,2048]{2,1,0:T(8,128)} %copy-done.13) | copy-start | bytes 3145732
  143.8 2.8 %copy-start.16 = (f32[4,32,2048]{2,1,0:T(8,128)S(1)}, f32[4,32,2048]{2,1,0:T(8,128)}, u32[]{:S(2)}) copy-start(f32[4,32,2048]{2,1,0:T(8,128)} %get-tuple-element.13) | copy-start | bytes 3145732
  143.8 2.8 %copy-start.22 = (f32[4,4,32,32]{3,2,1,0:T(8,128)S(1)}, f32[4,4,32,32]{3,2,1,0:T(8,128)}, u32[]{:S(2)}) copy-start(f32[4,4,32,32]{3,2,1,0:T(8,128)} %fusion.16) | copy-start | bytes 196612
  146.6 1.3 copy-start.21
  203.2 2.2 copy-start.2
  203.5 3.2 %copy-start.5 = (bf16[16,32,2,2048]{3,1,0,2:T(8,128)(2,1)S(1)}, bf16[16,32,2,2048]{3,1,0,2:T(8,128)(2,1)}, u32[]{:S(2)}) copy-start(bf16[16,32,2,2048]{3,1,0,2:T(8,128)(2,1)} %copy-done.3) | copy-start | bytes 12582916
  206.0 2.4 %copy-start.7 = (bf16[16,32,2,2048]{3,1,0,2:T(8,128)(2,1)S(1)}, bf16[16,32,2,2048]{3,1,0,2:T(8,128)(2,1)}, u32[]{:S(2)}) copy-start(bf16[16,32,2,2048]{3,1,0,2:T(8,128)(2,1)} %copy-done.6) | copy-start | bytes 12582916
Sparse Core Ops, SparseCore 0:
  10.9 83.4 all-gather.3
  154.5 44.8 all-gather.5
